TPU v7x, 256 devices: a whole 4x4x8 slice. The times are simulated.
256 devices in a mesh: seq: 16 (over x, y_hi, core), fsdp: 16 (over z, y_lo).
Axes of the slice: x: 4, y: 4 (y_hi: 2, y_lo: 2; y = y_hi * 2 + y_lo), z: 8, core: 2. Of those that a mesh axis runs over, the one named last changes fastest.
Arguments:
- hidden: bfloat16 [32768, 8192], P(('seq', 'fsdp')), may hold values from -24 to 24
- kv_blocks: bfloat16 [8192, 1024], P('fsdp'), may hold values from -0.0625 to 0.0625
- kv_scale: float32 [64, 8], P('fsdp'), may hold values from 0.5 to 2
- queries: bfloat16 [32768, 4096], P(('seq', 'fsdp')), may hold values from -24 to 24
- grad_out: bfloat16 [32768, 4096], P(('seq', 'fsdp')), may hold values from -6 to 6
Outputs:
- attn_out: bfloat16 [32768, 4096], P(('seq', 'fsdp'))
- grad_queries: bfloat16 [32768, 4096], P(('seq', 'fsdp'))
- grad_hidden: bfloat16 [32768, 8192], P(('seq', 'fsdp'))
- weight_grad: float32 [8192, 1024], P('fsdp')
All inputs are finite; a program needn't handle non-finite values.
Results may differ from a plain program's by a relative error of at most 0.0075.
The roundings to bfloat16 on the way count: a program that leaves them out, or rounds other values in their place, can miss the bound.
Values may be sent and summed in bfloat16 or wider, within the bound.
No kernel may reach another device: no remote copies, remote signals or barrier semaphores. Data moves between devices by JAX's collectives and lax.ppermute only.
A program may use at most 128 MiB of HBM per device.

v0:
```python
import jax
import jax.numpy as jnp
from jax import lax
from jax.sharding import Mesh
from jax.sharding import PartitionSpec as P

HEADS = 32
KV_HEADS = 4
HEAD = 128
QB = 128
FSDP = ("fsdp_0", "fsdp_1")
SEQ_FSDP = ("seq", "fsdp_0", "fsdp_1")
NEG = -1e30


def gather_axes(value, axes, dim):
    if not axes:
        return value
    nearer = lax.all_gather(value, axes[-1], axis=dim, tiled=True)
    return gather_axes(nearer, axes[:-1], dim)


def shifted(block, axis, distance):
    devices = range(lax.axis_size(axis))
    route = [(i - distance, i) for i in devices if i - distance in devices]
    return lax.ppermute(block, axis, route)


def dequantize(blocks, scale):
    rows, cols = blocks.shape
    grid = blocks.astype(jnp.float32).reshape(scale.shape[0], QB, scale.shape[1], QB)
    return (grid * scale[:, None, :, None]).reshape(rows, cols).astype(jnp.bfloat16)


def attend_group(operands, allowed):
    qgrp, kgrp, vgrp, ggrp = operands
    factor = 1.0 / float(HEAD) ** 0.5
    scores = jnp.einsum("rhd,kd->rhk", qgrp, kgrp, preferred_element_type=jnp.float32) * factor
    scores = jnp.where(allowed[:, None, :], scores, NEG)
    top = jnp.max(scores, axis=-1, keepdims=True)
    expd = jnp.exp(scores - top)
    probs = expd / jnp.sum(expd, axis=-1, keepdims=True)
    probs_b = probs.astype(jnp.bfloat16)
    output = jnp.einsum("rhk,kd->rhd", probs_b, vgrp, preferred_element_type=jnp.float32).astype(
        jnp.bfloat16
    )
    dprobs = jnp.einsum("rhd,kd->rhk", ggrp, vgrp, preferred_element_type=jnp.float32)
    delta = jnp.sum(probs * dprobs, axis=-1, keepdims=True)
    dscores = (probs * (dprobs - delta) * factor).astype(jnp.bfloat16)
    gradq = jnp.einsum("rhk,kd->rhd", dscores, kgrp, preferred_element_type=jnp.float32).astype(
        jnp.bfloat16
    )
    gradk = jnp.einsum("rhk,rhd->kd", dscores, qgrp, preferred_element_type=jnp.float32)
    gradv = jnp.einsum("rhk,rhd->kd", probs_b, ggrp, preferred_element_type=jnp.float32)
    return (output, gradq, gradk, gradv)


def attend(queries, window, grad_out, allowed):
    rows = queries.shape[0]
    count = window.shape[0]
    group = HEADS // KV_HEADS
    kvw = KV_HEADS * HEAD
    qgrp = queries.reshape(rows, KV_HEADS, group, HEAD).transpose(1, 0, 2, 3)
    ggrp = grad_out.reshape(rows, KV_HEADS, group, HEAD).transpose(1, 0, 2, 3)
    kgrp = window[:, :kvw].reshape(count, KV_HEADS, HEAD).transpose(1, 0, 2)
    vgrp = window[:, kvw:].reshape(count, KV_HEADS, HEAD).transpose(1, 0, 2)
    output, gradq, gradk, gradv = lax.map(
        lambda ops: attend_group(ops, allowed), (qgrp, kgrp, vgrp, ggrp)
    )
    output = output.transpose(1, 0, 2, 3).reshape(rows, HEADS * HEAD)
    gradq = gradq.transpose(1, 0, 2, 3).reshape(rows, HEADS * HEAD)
    gradk = gradk.transpose(1, 0, 2).reshape(count, kvw)
    gradv = gradv.transpose(1, 0, 2).reshape(count, kvw)
    return (output, gradq, jnp.concatenate([gradk, gradv], axis=1))


def body(hidden, kv_blocks, kv_scale, queries, grad_out):
    tok = hidden.shape[0]
    groups = lax.axis_size(FSDP)
    reach = groups // 2
    place = lax.axis_index(FSDP)
    linear = lax.axis_index("seq") * groups + place
    weights = dequantize(kv_blocks, kv_scale)
    columns = lax.all_to_all(hidden, FSDP, split_axis=1, concat_axis=0, tiled=True)
    whole = gather_axes(weights, FSDP, 0)
    kv = jnp.dot(hidden, whole, preferred_element_type=jnp.float32).astype(jnp.bfloat16)
    pieces = []
    for offset in range(reach, 0, -1):
        pieces.append(shifted(kv, SEQ_FSDP, offset))
    window = jnp.concatenate(pieces + [kv], axis=0)
    base = linear * tok
    qpos = base + jnp.arange(tok, dtype=jnp.int32)
    kpos = base - reach * tok + jnp.arange((reach + 1) * tok, dtype=jnp.int32)
    span = reach * tok
    allowed = (
        (qpos[:, None] - kpos[None, :] < span)
        & (kpos[None, :] <= qpos[:, None])
        & (kpos[None, :] >= 0)
    )
    attn_out, grad_queries, dwin = attend(queries, window, grad_out, allowed)
    total = dwin[reach * tok :]
    inside = total
    for offset in range(1, reach + 1):
        piece = dwin[(reach - offset) * tok : (reach - offset + 1) * tok]
        returned = shifted(piece, SEQ_FSDP, -offset)
        total = total + returned
        inside = inside + jnp.where(place + offset < groups, returned, jnp.zeros_like(returned))
    all_grad = total.astype(jnp.bfloat16)
    seg_grad = inside.astype(jnp.bfloat16)
    grad_hidden = lax.dot_general(
        seg_grad, whole, (((1,), (1,)), ((), ())), preferred_element_type=jnp.float32
    ).astype(jnp.bfloat16)
    shard_grad = lax.dot_general(
        columns,
        lax.all_gather(all_grad, FSDP, axis=0, tiled=True),
        (((0,), (0,)), ((), ())),
        preferred_element_type=jnp.float32,
    )
    weight_grad = lax.psum(shard_grad, "seq")
    return (attn_out, grad_queries, grad_hidden, weight_grad)


def solution(mesh):
    finer = Mesh(mesh.devices.reshape(mesh.shape["seq"], 8, 2), ("seq", "fsdp_0", "fsdp_1"))
    placed = (P(SEQ_FSDP, None), P(FSDP, None), P(FSDP, None), P(SEQ_FSDP, None), P(SEQ_FSDP, None))
    return jax.shard_map(
        body,
        mesh=finer,
        in_specs=placed,
        out_specs=(P(SEQ_FSDP, None), P(SEQ_FSDP, None), P(SEQ_FSDP, None), P(FSDP, None)),
        check_vma=False,
    )
```

profile of v0, /device:TPU:1, one launch (start us, length us, event | category | flops | bytes accessed | tf_op | source)
XLA Modules:
  0.0 1012.2 jit_solution(2476808071577137936)
XLA Ops:
  10.0 42.4 %all-gather.4.cloned.1.call-done = bf16[1024,1024]{1,0:T(8,128)(2,1)} async-done(((bf16[512,1024]{1,0:T(8,128)(2,1)}), bf16[1024,1024]{1,0:T(8,128)(2,1)}) %all-gather.4.cloned.1.call-update) | async-done | bytes 2097168 | tf_op jit(solution)/shard_map/all_gather | solution.py:19
  52.5 175.5 %all-gather.6.cloned.1.call-done = bf16[8192,1024]{1,0:T(8,128)(2,1)} async-done(((bf16[1024,1024]{1,0:T(8,128)(2,1)}), bf16[8192,1024]{1,0:T(8,128)(2,1)}) %all-gather.6.cloned.1.call-update) | async-done | bytes 16777232 | tf_op jit(solution)/shard_map/all_gather | solution.py:19
  228.0 8.1 fusion.100
  236.1 4.7 collective-permute-start
  240.8 4.1 collective-permute-start.1
  245.0 5.8 collective-permute-start.2
  250.8 2.3 copy.31
  253.1 2.3 copy.34
  255.4 5.0 collective-permute-start.3
  260.3 2.3 collective-permute-start.4
  262.7 5.3 collective-permute-start.5
  269.0 2.6 collective-permute-start.6
  271.7 18.8 %collective-permute-done.2 = bf16[128,1024]{1,0:T(8,128)(2,1)S(1)} collective-permute-done((bf16[128,1024]{1,0:T(8,128)(2,1)S(1)}, bf16[128,1024]{1,0:T(8,128)(2,1)S(1)}, u32[]{:S(2)}, u32[]{:S(2)}) %collective-permute-start.2) | collective-permute-done | bytes 262176 | tf_op jit(solution)/shard_map/ppermute | solution.py:26
  290.5 1.9 collective-permute-start.7
  292.5 13.1 %collective-permute-done.3 = bf16[128,1024]{1,0:T(8,128)(2,1)S(1)} collective-permute-done((bf16[128,1024]{1,0:T(8,128)(2,1)S(1)}, bf16[128,1024]{1,0:T(8,128)(2,1)S(1)}, u32[]{:S(2)}, u32[]{:S(2)}) %collective-permute-start.3) | collective-permute-done | bytes 262176 | tf_op jit(solution)/shard_map/ppermute | solution.py:26
  305.6 7.8 collective-permute-done.5
  313.4 8.5 collective-permute-done.6
  321.9 12.2 %collective-permute-done.7 = bf16[128,1024]{1,0:T(8,128)(2,1)S(1)} collective-permute-done((bf16[128,1024]{1,0:T(8,128)(2,1)S(1)}, bf16[128,1024]{1,0:T(8,128)(2,1)S(1)}, u32[]{:S(2)}, u32[]{:S(2)}) %collective-permute-start.7) | collective-permute-done | bytes 262176 | tf_op jit(solution)/shard_map/ppermute | solution.py:26
  336.1 180.6 %while.17 = (s32[]{:T(128)}, bf16[4,128,8,128]{3,1,2,0:T(8,128)(2,1)}, bf16[4,128,8,128]{3,1,2,0:T(8,128)(2,1)}, f32[4,1152,128]{1,2,0:T(8,128)S(1)}, f32[4,1152...) while((s32[]{:T(128)}, ...), condition=%wide.region_4.5_spmd.clone, body=%wide.region_0.4_spmd.clone.sunk | while | flops 2449958400 | bytes 52865276 | solution.py:67
  337.0 5.7 exponential_reduce_fusion.2
  342.7 4.0 fusion.169
  346.7 12.1 %fusion.171 = f32[4,1152,128]{1,2,0:T(8,128)S(1)} fusion(f32[4,1152,128]{1,2,0:T(8,128)S(1)} %get-tuple-element.259, s32[]{:T(128)} %get-tuple-element.256, f32[128,8,1152]{2,0,1:T(8,128)} %fusion.169, bf16[4,128,8,128]{1,3,2,0:T(8,128)(2,1)} %get-tuple-element.274, f32[128,8,1152]{2,0,1:T(8,128)} %get-tuple-element.242, ...), kind=kOutput, calls=%fused_computation.17.clone.1 | convolution fusion | flops 310249600 | bytes 19735552 | tf_op jit(solution)/shard_map/while/body/eval_jaxpr/rhk,rhd->kd/dot_general | solution.py:53
  358.7 12.5 %fusion.170 = bf16[4,128,8,128]{3,1,2,0:T(8,128)(2,1)} fusion(bf16[4,128,8,128]{3,1,2,0:T(8,128)(2,1)} %get-tuple-element.258, s32[]{:T(128)} %get-tuple-element.256, f32[128,8,1152]{2,0,1:T(8,128)} %fusion.169, bf16[4,1152,128]{2,1,0:T(8,128)(2,1)} %get-tuple-element.275, f32[128,8,1152]{2,0,1:T(8,128)} %get-tuple-element.242, ...), kind=kOutput, calls=%fused_computation.28.clone.1 | convolution fusion | flops 310380672 | bytes 19440640 | tf_op jit(solution)/shard_map/while/body/eval_jaxpr/rhk,kd->rhd/dot_general | solution.py:50
  371.2 4.8 fusion.172
  376.1 5.1 fusion.168
  382.1 5.7 exponential_reduce_fusion.2
  387.8 4.0 fusion.169
  391.8 12.1 %fusion.171 = f32[4,1152,128]{1,2,0:T(8,128)S(1)} fusion(f32[4,1152,128]{1,2,0:T(8,128)S(1)} %get-tuple-element.259, s32[]{:T(128)} %get-tuple-element.256, f32[128,8,1152]{2,0,1:T(8,128)} %fusion.169, bf16[4,128,8,128]{1,3,2,0:T(8,128)(2,1)} %get-tuple-element.274, f32[128,8,1152]{2,0,1:T(8,128)} %get-tuple-element.242, ...), kind=kOutput, calls=%fused_computation.17.clone.1 | convolution fusion | flops 310249600 | bytes 19735552 | tf_op jit(solution)/shard_map/while/body/eval_jaxpr/rhk,rhd->kd/dot_general | solution.py:53
  403.9 12.5 %fusion.170 = bf16[4,128,8,128]{3,1,2,0:T(8,128)(2,1)} fusion(bf16[4,128,8,128]{3,1,2,0:T(8,128)(2,1)} %get-tuple-element.258, s32[]{:T(128)} %get-tuple-element.256, f32[128,8,1152]{2,0,1:T(8,128)} %fusion.169, bf16[4,1152,128]{2,1,0:T(8,128)(2,1)} %get-tuple-element.275, f32[128,8,1152]{2,0,1:T(8,128)} %get-tuple-element.242, ...), kind=kOutput, calls=%fused_computation.28.clone.1 | convolution fusion | flops 310380672 | bytes 19440640 | tf_op jit(solution)/shard_map/while/body/eval_jaxpr/rhk,kd->rhd/dot_general | solution.py:50
  416.4 4.8 fusion.172
  421.2 5.1 fusion.168
  427.3 5.7 exponential_reduce_fusion.2
  433.0 4.0 fusion.169
  437.0 12.1 %fusion.171 = f32[4,1152,128]{1,2,0:T(8,128)S(1)} fusion(f32[4,1152,128]{1,2,0:T(8,128)S(1)} %get-tuple-element.259, s32[]{:T(128)} %get-tuple-element.256, f32[128,8,1152]{2,0,1:T(8,128)} %fusion.169, bf16[4,128,8,128]{1,3,2,0:T(8,128)(2,1)} %get-tuple-element.274, f32[128,8,1152]{2,0,1:T(8,128)} %get-tuple-element.242, ...), kind=kOutput, calls=%fused_computation.17.clone.1 | convolution fusion | flops 310249600 | bytes 19735552 | tf_op jit(solution)/shard_map/while/body/eval_jaxpr/rhk,rhd->kd/dot_general | solution.py:53
  449.0 12.5 %fusion.170 = bf16[4,128,8,128]{3,1,2,0:T(8,128)(2,1)} fusion(bf16[4,128,8,128]{3,1,2,0:T(8,128)(2,1)} %get-tuple-element.258, s32[]{:T(128)} %get-tuple-element.256, f32[128,8,1152]{2,0,1:T(8,128)} %fusion.169, bf16[4,1152,128]{2,1,0:T(8,128)(2,1)} %get-tuple-element.275, f32[128,8,1152]{2,0,1:T(8,128)} %get-tuple-element.242, ...), kind=kOutput, calls=%fused_computation.28.clone.1 | convolution fusion | flops 310380672 | bytes 19440640 | tf_op jit(solution)/shard_map/while/body/eval_jaxpr/rhk,kd->rhd/dot_general | solution.py:50
  461.6 4.8 fusion.172
  466.4 5.1 fusion.168
  472.4 5.7 exponential_reduce_fusion.2
  478.2 4.0 fusion.169
  482.1 12.1 %fusion.171 = f32[4,1152,128]{1,2,0:T(8,128)S(1)} fusion(f32[4,1152,128]{1,2,0:T(8,128)S(1)} %get-tuple-element.259, s32[]{:T(128)} %get-tuple-element.256, f32[128,8,1152]{2,0,1:T(8,128)} %fusion.169, bf16[4,128,8,128]{1,3,2,0:T(8,128)(2,1)} %get-tuple-element.274, f32[128,8,1152]{2,0,1:T(8,128)} %get-tuple-element.242, ...), kind=kOutput, calls=%fused_computation.17.clone.1 | convolution fusion | flops 310249600 | bytes 19735552 | tf_op jit(solution)/shard_map/while/body/eval_jaxpr/rhk,rhd->kd/dot_general | solution.py:53
  494.2 12.5 %fusion.170 = bf16[4,128,8,128]{3,1,2,0:T(8,128)(2,1)} fusion(bf16[4,128,8,128]{3,1,2,0:T(8,128)(2,1)} %get-tuple-element.258, s32[]{:T(128)} %get-tuple-element.256, f32[128,8,1152]{2,0,1:T(8,128)} %fusion.169, bf16[4,1152,128]{2,1,0:T(8,128)(2,1)} %get-tuple-element.275, f32[128,8,1152]{2,0,1:T(8,128)} %get-tuple-element.242, ...), kind=kOutput, calls=%fused_computation.28.clone.1 | convolution fusion | flops 310380672 | bytes 19440640 | tf_op jit(solution)/shard_map/while/body/eval_jaxpr/rhk,kd->rhd/dot_general | solution.py:50
  506.7 4.8 fusion.172
  511.6 5.1 fusion.168
  516.7 2.0 fusion.103
  518.7 1.9 collective-permute-start.10
  520.6 4.6 collective-permute-start.11
  525.2 5.8 collective-permute-start.12
  531.0 2.0 collective-permute-start.13
  533.0 1.9 collective-permute-start.14
  536.8 17.9 %collective-permute-start.15 = (f32[128,1024]{0,1:T(8,128)S(1)}, f32[128,1024]{0,1:T(8,128)S(1)}, u32[]{:S(2)}, u32[]{:S(2)}) collective-permute-start(f32[128,1024]{0,1:T(8,128)S(1)} %get-tuple-element.160), channel_id=1, source_target_pairs={{8,0},{9,1},{10,2},{11,3},{12,4},{13,5},{14,6},{15,7},{16,8},{17,9... | collective-permute-start | bytes 1572872 | tf_op jit(solution)/shard_map/ppermute | solution.py:26
  554.7 15.7 %collective-permute-done.11 = f32[128,1024]{0,1:T(8,128)S(1)} collective-permute-done((f32[128,1024]{0,1:T(8,128)S(1)}, f32[128,1024]{0,1:T(8,128)S(1)}, u32[]{:S(2)}, u32[]{:S(2)}) %collective-permute-start.11) | collective-permute-done | bytes 524320 | tf_op jit(solution)/shard_map/ppermute | solution.py:26
  570.5 17.8 %collective-permute-start.8 = (f32[128,1024]{0,1:T(8,128)S(1)}, f32[128,1024]{0,1:T(8,128)S(1)}, u32[]{:S(2)}, u32[]{:S(2)}) collective-permute-start(f32[128,1024]{0,1:T(8,128)S(1)} %get-tuple-element.154), channel_id=1, source_target_pairs={{1,0},{2,1},{3,2},{4,3},{5,4},{6,5},{7,6},{8,7},{9,8},{10,9},{11,1... | collective-permute-start | bytes 1572872 | tf_op jit(solution)/shard_map/ppermute | solution.py:26
  588.3 13.7 %collective-permute-start.9 = (f32[128,1024]{0,1:T(8,128)S(1)}, f32[128,1024]{0,1:T(8,128)S(1)}, u32[]{:S(2)}, u32[]{:S(2)}) collective-permute-start(f32[128,1024]{0,1:T(8,128)S(1)} %get-tuple-element.155), channel_id=1, source_target_pairs={{2,0},{3,1},{4,2},{5,3},{6,4},{7,5},{8,6},{9,7},{10,8},{11,9},{12,... | collective-permute-start | bytes 1572872 | tf_op jit(solution)/shard_map/ppermute | solution.py:26
  602.0 32.7 %collective-permute-done.13 = f32[128,1024]{0,1:T(8,128)S(1)} collective-permute-done((f32[128,1024]{0,1:T(8,128)S(1)}, f32[128,1024]{0,1:T(8,128)S(1)}, u32[]{:S(2)}, u32[]{:S(2)}) %collective-permute-start.13) | collective-permute-done | bytes 524320 | tf_op jit(solution)/shard_map/ppermute | solution.py:26
  634.7 7.5 collective-permute-done.14
  645.4 4.1 copy.41
  649.5 131.0 %all_to_all.19 = bf16[128,16,512]{0,2,1:T(8,128)(2,1)} all-to-all(bf16[128,16,512]{0,2,1:T(8,128)(2,1)} %bitcast.168), channel_id=1, replica_groups=mesh['seq'=16,'fsdp_0'=8,'fsdp_1'=2] {'fsdp_0','fsdp_1'}, dimensions={1} | all-to-all | bytes 4194304 | tf_op jit(solution)/shard_map/all_to_all | solution.py:84
  780.5 3.9 copy.42
  784.4 56.0 %all-gather.8.cloned.1.call-done = bf16[2048,1024]{0,1:T(8,128)(2,1)} async-done(((bf16[128,1024]{0,1:T(8,128)(2,1)}), bf16[2048,1024]{0,1:T(8,128)(2,1)}) %all-gather.8.cloned.1.call-update) | async-done | bytes 4194320 | tf_op jit(solution)/shard_map/all_gather | solution.py:115
  840.5 6.5 convolution_bitcast_fusion.2
  847.0 2.0 copy.38
  852.6 13.9 %convolution_convert_fusion.1 = bf16[128,8192]{1,0:T(8,128)(2,1)} fusion(bf16[8192,1024]{1,0:T(8,128)(2,1)} %all-gather.6.cloned.1.call-done, f32[128,1024]{0,1:T(8,128)} %copy-done.5, f32[128,1024]{0,1:T(8,128)} %copy-done.4, f32[128,1024]{0,1:T(8,128)} %copy-done.3, f32[128,1024]{0,1:T(8,128)} %copy-done.2, f32[128,1024]{0,1:T(8,128)S(1)} %collective-permute-done.11, ...), kind=kOutput, calls=%fused_computation.83 | convolution fusion | flops 2150891520 | bytes 27787272 | tf_op jit(solution)/shard_map/dot_general | solution.py:110
  866.5 136.3 %all-reduce.2.cloned.1.call-done = f32[512,1024]{0,1:T(8,128)} async-done(((f32[512,1024]{0,1:T(8,128)}), f32[512,1024]{0,1:T(8,128)}) %all-reduce.2.cloned.1.call-update) | async-done | bytes 2097168 | tf_op jit(solution)/shard_map/psum | solution.py:119
  1002.8 2.9 copy.43
  (64 shorter events, 17.9 us)
Async XLA Ops:
  7.2 1.2 copy-start.9
  7.2 45.2 %all-gather.4.cloned.1.call-start = ((), (), s32[]{:S(2)}) async-start(), calls=%async_computation.1 | async-start | bytes 3145728 | tf_op jit(solution)/shard_map/all_gather | solution.py:19
  10.0 218.0 %copy-start.1 = (bf16[128,8192]{1,0:T(8,128)(2,1)S(1)}, bf16[128,8192]{1,0:T(8,128)(2,1)}, u32[]{:S(2)}) copy-start(bf16[128,8192]{1,0:T(8,128)(2,1)} %param.7) | copy-start | bytes 6291460
  10.0 218.0 %all-gather.6.cloned.1.call-start = ((), (), s32[]{:S(2)}) async-start(), calls=%async_computation.2 | async-start | bytes 18874368 | tf_op jit(solution)/shard_map/all_gather | solution.py:19
  52.4 788.0 %all-gather.8.cloned.1.call-start = ((), (), s32[]{:S(2)}) async-start(), calls=%async_computation.3 | async-start | bytes 4456448 | tf_op jit(solution)/shard_map/all_gather | solution.py:115
  236.1 26.6 %collective-permute-start = (bf16[128,1024]{1,0:T(8,128)(2,1)S(1)}, bf16[128,1024]{1,0:T(8,128)(2,1)}, u32[]{:S(2)}, u32[]{:S(2)}) collective-permute-start(bf16[128,1024]{1,0:T(8,128)(2,1)S(1)} %fusion.100), channel_id=1, source_target_pairs={{0,8},{1,9},{2,10},{3,11},{4,12},{5,13},{6,14},{7,15},{8,16},{9,17... | collective-permute-start | bytes 786440 | tf_op jit(solution)/shard_map/ppermute | solution.py:26
  240.8 28.2 %collective-permute-start.1 = (bf16[128,1024]{1,0:T(8,128)(2,1)S(1)}, bf16[128,1024]{1,0:T(8,128)(2,1)S(1)}, u32[]{:S(2)}, u32[]{:S(2)}) collective-permute-start(bf16[128,1024]{1,0:T(8,128)(2,1)S(1)} %fusion.100), channel_id=1, source_target_pairs={{0,7},{1,8},{2,9},{3,10},{4,11},{5,12},{6,13},{7,14},{8,15},{9,16}... | collective-permute-start | bytes 786440 | tf_op jit(solution)/shard_map/ppermute | solution.py:26
  245.0 45.6 %collective-permute-start.2 = (bf16[128,1024]{1,0:T(8,128)(2,1)S(1)}, bf16[128,1024]{1,0:T(8,128)(2,1)S(1)}, u32[]{:S(2)}, u32[]{:S(2)}) collective-permute-start(bf16[128,1024]{1,0:T(8,128)(2,1)S(1)} %fusion.100), channel_id=1, source_target_pairs={{0,6},{1,7},{2,8},{3,9},{4,10},{5,11},{6,12},{7,13},{8,14},{9,15},... | collective-permute-start | bytes 786440 | tf_op jit(solution)/shard_map/ppermute | solution.py:26
  255.4 50.2 %collective-permute-start.3 = (bf16[128,1024]{1,0:T(8,128)(2,1)S(1)}, bf16[128,1024]{1,0:T(8,128)(2,1)S(1)}, u32[]{:S(2)}, u32[]{:S(2)}) collective-permute-start(bf16[128,1024]{1,0:T(8,128)(2,1)S(1)} %fusion.100), channel_id=1, source_target_pairs={{0,5},{1,6},{2,7},{3,8},{4,9},{5,10},{6,11},{7,12},{8,13},{9,14},{... | collective-permute-start | bytes 786440 | tf_op jit(solution)/shard_map/ppermute | solution.py:26
  260.3 45.2 %collective-permute-start.4 = (bf16[128,1024]{1,0:T(8,128)(2,1)S(1)}, bf16[128,1024]{1,0:T(8,128)(2,1)S(1)}, u32[]{:S(2)}, u32[]{:S(2)}) collective-permute-start(bf16[128,1024]{1,0:T(8,128)(2,1)S(1)} %fusion.100), channel_id=1, source_target_pairs={{0,4},{1,5},{2,6},{3,7},{4,8},{5,9},{6,10},{7,11},{8,12},{9,13},{1... | collective-permute-start | bytes 786440 | tf_op jit(solution)/shard_map/ppermute | solution.py:26
  262.7 50.7 %collective-permute-start.5 = (bf16[128,1024]{1,0:T(8,128)(2,1)S(1)}, bf16[128,1024]{1,0:T(8,128)(2,1)S(1)}, u32[]{:S(2)}, u32[]{:S(2)}) collective-permute-start(bf16[128,1024]{1,0:T(8,128)(2,1)S(1)} %fusion.100), channel_id=1, source_target_pairs={{0,3},{1,4},{2,5},{3,6},{4,7},{5,8},{6,9},{7,10},{8,11},{9,12},{10... | collective-permute-start | bytes 786440 | tf_op jit(solution)/shard_map/ppermute | solution.py:26
  269.0 52.8 %collective-permute-start.6 = (bf16[128,1024]{1,0:T(8,128)(2,1)S(1)}, bf16[128,1024]{1,0:T(8,128)(2,1)S(1)}, u32[]{:S(2)}, u32[]{:S(2)}) collective-permute-start(bf16[128,1024]{1,0:T(8,128)(2,1)S(1)} %fusion.100), channel_id=1, source_target_pairs={{0,2},{1,3},{2,4},{3,5},{4,6},{5,7},{6,8},{7,9},{8,10},{9,11},{10,... | collective-permute-start | bytes 786440 | tf_op jit(solution)/shard_map/ppermute | solution.py:26
  290.5 43.6 %collective-permute-start.7 = (bf16[128,1024]{1,0:T(8,128)(2,1)S(1)}, bf16[128,1024]{1,0:T(8,128)(2,1)S(1)}, u32[]{:S(2)}, u32[]{:S(2)}) collective-permute-start(bf16[128,1024]{1,0:T(8,128)(2,1)S(1)} %fusion.100), channel_id=1, source_target_pairs={{0,1},{1,2},{2,3},{3,4},{4,5},{5,6},{6,7},{7,8},{8,9},{9,10},{10,1... | collective-permute-start | bytes 786440 | tf_op jit(solution)/shard_map/ppermute | solution.py:26
  516.7 127.6 %copy-start = (f32[4,1152,128]{1,2,0:T(8,128)S(1)}, f32[4,1152,128]{1,2,0:T(8,128)}, u32[]{:S(2)}) copy-start(f32[4,1152,128]{1,2,0:T(8,128)} %get-tuple-element.62) | copy-start | bytes 7077892
  518.7 18.1 %collective-permute-start.10 = (f32[128,1024]{0,1:T(8,128)S(1)}, f32[128,1024]{0,1:T(8,128)S(1)}, u32[]{:S(2)}, u32[]{:S(2)}) collective-permute-start(f32[128,1024]{0,1:T(8,128)S(1)} %get-tuple-element.156), channel_id=1, source_target_pairs={{3,0},{4,1},{5,2},{6,3},{7,4},{8,5},{9,6},{10,7},{11,8},{12,9},{13... | collective-permute-start | bytes 1572872 | tf_op jit(solution)/shard_map/ppermute | solution.py:26
  520.6 49.9 %collective-permute-start.11 = (f32[128,1024]{0,1:T(8,128)S(1)}, f32[128,1024]{0,1:T(8,128)S(1)}, u32[]{:S(2)}, u32[]{:S(2)}) collective-permute-start(f32[128,1024]{0,1:T(8,128)S(1)} %get-tuple-element.157), channel_id=1, source_target_pairs={{4,0},{5,1},{6,2},{7,3},{8,4},{9,5},{10,6},{11,7},{12,8},{13,9},{1... | collective-permute-start | bytes 1572872 | tf_op jit(solution)/shard_map/ppermute | solution.py:26
  525.2 63.1 %collective-permute-start.12 = (f32[128,1024]{0,1:T(8,128)S(1)}, f32[128,1024]{0,1:T(8,128)S(1)}, u32[]{:S(2)}, u32[]{:S(2)}) collective-permute-start(f32[128,1024]{0,1:T(8,128)S(1)} %get-tuple-element.158), channel_id=1, source_target_pairs={{5,0},{6,1},{7,2},{8,3},{9,4},{10,5},{11,6},{12,7},{13,8},{14,9},{... | collective-permute-start | bytes 1572872 | tf_op jit(solution)/shard_map/ppermute | solution.py:26
  531.0 103.8 %collective-permute-start.13 = (f32[128,1024]{0,1:T(8,128)S(1)}, f32[128,1024]{0,1:T(8,128)S(1)}, u32[]{:S(2)}, u32[]{:S(2)}) collective-permute-start(f32[128,1024]{0,1:T(8,128)S(1)} %get-tuple-element.159), channel_id=1, source_target_pairs={{6,0},{7,1},{8,2},{9,3},{10,4},{11,5},{12,6},{13,7},{14,8},{15,9},... | collective-permute-start | bytes 1572872 | tf_op jit(solution)/shard_map/ppermute | solution.py:26
  533.0 109.3 %collective-permute-start.14 = (f32[128,1024]{0,1:T(8,128)S(1)}, f32[128,1024]{0,1:T(8,128)S(1)}, u32[]{:S(2)}, u32[]{:S(2)}) collective-permute-start(f32[128,1024]{0,1:T(8,128)S(1)} %get-tuple-element.161), channel_id=1, source_target_pairs={{7,0},{8,1},{9,2},{10,3},{11,4},{12,5},{13,6},{14,7},{15,8},{16,9}... | collective-permute-start | bytes 1572872 | tf_op jit(solution)/shard_map/ppermute | solution.py:26
  536.8 105.5 %collective-permute-start.15 = (f32[128,1024]{0,1:T(8,128)S(1)}, f32[128,1024]{0,1:T(8,128)S(1)}, u32[]{:S(2)}, u32[]{:S(2)}) collective-permute-start(f32[128,1024]{0,1:T(8,128)S(1)} %get-tuple-element.160), channel_id=1, source_target_pairs={{8,0},{9,1},{10,2},{11,3},{12,4},{13,5},{14,6},{15,7},{16,8},{17,9... | collective-permute-start | bytes 1572872 | tf_op jit(solution)/shard_map/ppermute | solution.py:26
  570.5 71.8 %collective-permute-start.8 = (f32[128,1024]{0,1:T(8,128)S(1)}, f32[128,1024]{0,1:T(8,128)S(1)}, u32[]{:S(2)}, u32[]{:S(2)}) collective-permute-start(f32[128,1024]{0,1:T(8,128)S(1)} %get-tuple-element.154), channel_id=1, source_target_pairs={{1,0},{2,1},{3,2},{4,3},{5,4},{6,5},{7,6},{8,7},{9,8},{10,9},{11,1... | collective-permute-start | bytes 1572872 | tf_op jit(solution)/shard_map/ppermute | solution.py:26
  588.3 54.0 %copy-start.2 = (f32[128,1024]{0,1:T(8,128)}, f32[128,1024]{0,1:T(8,128)S(1)}, u32[]{:S(2)}) copy-start(f32[128,1024]{0,1:T(8,128)S(1)} %collective-permute-done.12) | copy-start | bytes 1572868
  588.3 54.0 %collective-permute-start.9 = (f32[128,1024]{0,1:T(8,128)S(1)}, f32[128,1024]{0,1:T(8,128)S(1)}, u32[]{:S(2)}, u32[]{:S(2)}) collective-permute-start(f32[128,1024]{0,1:T(8,128)S(1)} %get-tuple-element.155), channel_id=1, source_target_pairs={{2,0},{3,1},{4,2},{5,3},{6,4},{7,5},{8,6},{9,7},{10,8},{11,9},{12,... | collective-permute-start | bytes 1572872 | tf_op jit(solution)/shard_map/ppermute | solution.py:26
  634.7 7.6 copy-start.3
  642.3 0.8 copy-start.4
  642.3 1.0 copy-start.5
  642.3 1.2 copy-start.6
  643.5 0.8 copy-start.7
  645.4 357.4 %all-reduce.2.cloned.1.call-start = ((), (), s32[]{:S(2)}) async-start(), calls=%async_computation.4 | async-start | bytes 4194304 | tf_op jit(solution)/shard_map/psum | solution.py:119
  847.0 3.4 copy-start.8
Sparse Core Ops, SparseCore 0:
  10.4 41.9 all-gather.3
  54.2 173.7 all-gather.5
  645.5 194.9 all-gather.7
  847.1 155.5 all-reduce.1
where the time goes:
time: 1010 us
  waiting for transfers between devices  529 us (52%)
  matrix products  206 us (20%)
  blocking collectives  131 us (13%)
  starting transfers between devices  97.6 us (10%)
  local copies, waits for them, and re-layouts  27.1 us (3%)
  between operations  14.2 us (1%)
    all_gather x2, waiting for transfers between devices, gather_axes(): nearer = lax.all_gather(value, axes[-1], axis=dim, tiled=True)  218 us
    psum x1, waiting for transfers between devices, body(): weight_grad = lax.psum(shard_grad, 'seq')  136 us
    all_to_all x1, blocking collectives, body(): lax.all_to_all(hidden, FSDP, split_axis=1, concat_axis=0, tiled=True)  131 us
    ppermute x16, waiting for transfers between devices, shifted(): return lax.ppermute(block, axis, route)  118 us
    ppermute x16, starting transfers between devices, shifted(): return lax.ppermute(block, axis, route)  97.5 us
    all_gather x1, waiting for transfers between devices, body(): lax.all_gather(all_grad, FSDP, axis=0, tiled=True)  56 us
    dot_general x4, matrix products, attend_group(): jnp.einsum('rhk,kd->rhd', dscores, kgrp, preferred_element_type=jnp.float32)  50.1 us
    dot_general x4, matrix products, attend_group(): jnp.einsum('rhk,rhd->kd', dscores, qgrp, preferred_element_type=jnp.float32)  48.3 us
  transfers between devices with their start and end apart: 20, of which 13 were waited for; matrix products, arithmetic and copies ran while one was open for 3% of the time, Pallas kernels for 0%

commit v1 on v0

--- a/solution.py
+++ b/solution.py
@@ -112,7 +112,9 @@
     ).astype(jnp.bfloat16)
     shard_grad = lax.dot_general(
         columns,
-        lax.all_gather(all_grad, FSDP, axis=0, tiled=True),
+        jnp.concatenate(
+            lax.all_to_all(jnp.stack([all_grad] * lax.axis_size(FSDP)), FSDP, 0, 0), axis=0
+        ),
         (((0,), (0,)), ((), ())),
         preferred_element_type=jnp.float32,
     )

time: 1010 us -> 1010 us (level)
  waiting for transfers between devices: 529 us -> 492 us
  blocking collectives: 131 us -> 163 us
    all_gather x1 -> x0, waiting for transfers between devices: 56 us -> none  [body(): lax.all_gather(all_grad, FSDP, axis=0, tiled=True)]
    all_to_all x1, blocking collectives: 131 us -> 163 us  [body(): lax.all_to_all(jnp.stack([all_grad] * lax.axis_size(FSDP)), FSDP, 0, 0)]
    all_gather x2, waiting for transfers between devices: 218 us -> 249 us  [gather_axes(): nearer = lax.all_gather(value, axes[-1], axis=dim, tiled=True)]
    psum x1, waiting for transfers between devices: 136 us -> 125 us  [body(): weight_grad = lax.psum(shard_grad, 'seq')]
  transfers between devices with their start and end apart: 20 -> 20, of which waited for: 13 -> 12; matrix products, arithmetic and copies ran while one was open for 3% -> 22% of each run, Pallas kernels for 0% -> 0%
where the time goes in v1:
time: 1010 us
  waiting for transfers between devices  492 us (49%)
  matrix products  205 us (20%)
  blocking collectives  163 us (16%)
  starting transfers between devices  104 us (10%)
  local copies, waits for them, and re-layouts  27.1 us (3%)
  between operations  14.2 us (1%)
    all_gather x2, waiting for transfers between devices, gather_axes(): nearer = lax.all_gather(value, axes[-1], axis=dim, tiled=True)  249 us
    all_to_all x1, blocking collectives, body(): lax.all_to_all(jnp.stack([all_grad] * lax.axis_size(FSDP)), FSDP, 0, 0)  163 us
    psum x1, waiting for transfers between devices, body(): weight_grad = lax.psum(shard_grad, 'seq')  125 us
    ppermute x16, waiting for transfers between devices, shifted(): return lax.ppermute(block, axis, route)  119 us
    ppermute x16, starting transfers between devices, shifted(): return lax.ppermute(block, axis, route)  97.1 us
    dot_general x4, matrix products, attend_group(): jnp.einsum('rhk,kd->rhd', dscores, kgrp, preferred_element_type=jnp.float32)  50.4 us
    dot_general x4, matrix products, attend_group(): jnp.einsum('rhk,rhd->kd', dscores, qgrp, preferred_element_type=jnp.float32)  48.5 us
    sub x4, matrix products, attend_group(): expd = jnp.exp(scores - top)  23 us
  transfers between devices with their start and end apart: 20, of which 12 were waited for; matrix products, arithmetic and copies ran while one was open for 22% of the time, Pallas kernels for 0%

profile of v1, /device:TPU:1, one launch (start us, length us, event | category | flops | bytes accessed | tf_op | source)
XLA Modules:
  0.0 1013.3 jit_solution(11100136131444230876)
XLA Ops:
  10.0 42.4 %all-gather.3.cloned.1.call-done = bf16[1024,1024]{1,0:T(8,128)(2,1)} async-done(((bf16[512,1024]{1,0:T(8,128)(2,1)}), bf16[1024,1024]{1,0:T(8,128)(2,1)}) %all-gather.3.cloned.1.call-update) | async-done | bytes 2097168 | tf_op jit(solution)/shard_map/all_gather | solution.py:19
  52.5 2.4 copy.28
  54.9 3.9 copy.29
  58.8 6.9 all-to-all-start.1
  65.8 206.7 %all-gather.5.cloned.1.call-done = bf16[8192,1024]{1,0:T(8,128)(2,1)} async-done(((bf16[1024,1024]{1,0:T(8,128)(2,1)}), bf16[8192,1024]{1,0:T(8,128)(2,1)}) %all-gather.5.cloned.1.call-update) | async-done | bytes 16777232 | tf_op jit(solution)/shard_map/all_gather | solution.py:19
  272.4 8.1 fusion.105
  280.6 4.9 collective-permute-start
  285.5 3.9 collective-permute-start.1
  289.5 6.2 collective-permute-start.2
  295.7 2.3 copy.18
  298.0 2.3 copy.21
  300.2 4.6 collective-permute-start.3
  304.8 2.2 collective-permute-start.4
  307.0 5.7 collective-permute-start.5
  313.7 2.8 collective-permute-start.6
  316.5 18.6 %collective-permute-done.2 = bf16[128,1024]{1,0:T(8,128)(2,1)S(1)} collective-permute-done((bf16[128,1024]{1,0:T(8,128)(2,1)S(1)}, bf16[128,1024]{1,0:T(8,128)(2,1)S(1)}, u32[]{:S(2)}, u32[]{:S(2)}) %collective-permute-start.2) | collective-permute-done | bytes 262176 | tf_op jit(solution)/shard_map/ppermute | solution.py:26
  337.0 15.4 %collective-permute-done.3 = bf16[128,1024]{1,0:T(8,128)(2,1)S(1)} collective-permute-done((bf16[128,1024]{1,0:T(8,128)(2,1)S(1)}, bf16[128,1024]{1,0:T(8,128)(2,1)S(1)}, u32[]{:S(2)}, u32[]{:S(2)}) %collective-permute-start.3) | collective-permute-done | bytes 262176 | tf_op jit(solution)/shard_map/ppermute | solution.py:26
  352.5 5.8 collective-permute-done.5
  358.3 8.3 collective-permute-done.6
  366.6 12.2 %collective-permute-done.7 = bf16[128,1024]{1,0:T(8,128)(2,1)S(1)} collective-permute-done((bf16[128,1024]{1,0:T(8,128)(2,1)S(1)}, bf16[128,1024]{1,0:T(8,128)(2,1)S(1)}, u32[]{:S(2)}, u32[]{:S(2)}) %collective-permute-start.7) | collective-permute-done | bytes 262176 | tf_op jit(solution)/shard_map/ppermute | solution.py:26
  380.8 181.1 %while.17 = (s32[]{:T(128)}, bf16[4,128,8,128]{3,1,2,0:T(8,128)(2,1)}, bf16[4,128,8,128]{3,1,2,0:T(8,128)(2,1)}, f32[4,1152,128]{1,2,0:T(8,128)S(1)}, f32[4,1152...) while((s32[]{:T(128)}, ...), condition=%wide.region_4.5_spmd.clone, body=%wide.region_0.4_spmd.clone.sunk | while | flops 2449958400 | bytes 52865276 | solution.py:67
  381.7 5.7 exponential_reduce_fusion.2
  387.4 3.9 fusion.173
  391.4 12.1 %fusion.175 = f32[4,1152,128]{1,2,0:T(8,128)S(1)} fusion(f32[4,1152,128]{1,2,0:T(8,128)S(1)} %get-tuple-element.243, s32[]{:T(128)} %get-tuple-element.240, f32[128,8,1152]{2,0,1:T(8,128)} %fusion.173, bf16[4,128,8,128]{1,3,2,0:T(8,128)(2,1)} %get-tuple-element.258, f32[128,8,1152]{2,0,1:T(8,128)} %get-tuple-element.226, ...), kind=kOutput, calls=%fused_computation.17.clone.1 | convolution fusion | flops 310249600 | bytes 19735552 | tf_op jit(solution)/shard_map/while/body/eval_jaxpr/rhk,rhd->kd/dot_general | solution.py:53
  403.5 12.6 %fusion.174 = bf16[4,128,8,128]{3,1,2,0:T(8,128)(2,1)} fusion(bf16[4,128,8,128]{3,1,2,0:T(8,128)(2,1)} %get-tuple-element.242, s32[]{:T(128)} %get-tuple-element.240, f32[128,8,1152]{2,0,1:T(8,128)} %fusion.173, bf16[4,1152,128]{2,1,0:T(8,128)(2,1)} %get-tuple-element.259, f32[128,8,1152]{2,0,1:T(8,128)} %get-tuple-element.226, ...), kind=kOutput, calls=%fused_computation.28.clone.1 | convolution fusion | flops 310380672 | bytes 19440640 | tf_op jit(solution)/shard_map/while/body/eval_jaxpr/rhk,kd->rhd/dot_general | solution.py:50
  416.1 4.8 fusion.176
  421.0 5.1 fusion.172
  427.0 5.7 exponential_reduce_fusion.2
  432.7 3.9 fusion.173
  436.7 12.1 %fusion.175 = f32[4,1152,128]{1,2,0:T(8,128)S(1)} fusion(f32[4,1152,128]{1,2,0:T(8,128)S(1)} %get-tuple-element.243, s32[]{:T(128)} %get-tuple-element.240, f32[128,8,1152]{2,0,1:T(8,128)} %fusion.173, bf16[4,128,8,128]{1,3,2,0:T(8,128)(2,1)} %get-tuple-element.258, f32[128,8,1152]{2,0,1:T(8,128)} %get-tuple-element.226, ...), kind=kOutput, calls=%fused_computation.17.clone.1 | convolution fusion | flops 310249600 | bytes 19735552 | tf_op jit(solution)/shard_map/while/body/eval_jaxpr/rhk,rhd->kd/dot_general | solution.py:53
  448.8 12.6 %fusion.174 = bf16[4,128,8,128]{3,1,2,0:T(8,128)(2,1)} fusion(bf16[4,128,8,128]{3,1,2,0:T(8,128)(2,1)} %get-tuple-element.242, s32[]{:T(128)} %get-tuple-element.240, f32[128,8,1152]{2,0,1:T(8,128)} %fusion.173, bf16[4,1152,128]{2,1,0:T(8,128)(2,1)} %get-tuple-element.259, f32[128,8,1152]{2,0,1:T(8,128)} %get-tuple-element.226, ...), kind=kOutput, calls=%fused_computation.28.clone.1 | convolution fusion | flops 310380672 | bytes 19440640 | tf_op jit(solution)/shard_map/while/body/eval_jaxpr/rhk,kd->rhd/dot_general | solution.py:50
  461.4 4.9 fusion.176
  466.3 5.1 fusion.172
  472.3 5.7 exponential_reduce_fusion.2
  478.0 3.9 fusion.173
  482.0 12.1 %fusion.175 = f32[4,1152,128]{1,2,0:T(8,128)S(1)} fusion(f32[4,1152,128]{1,2,0:T(8,128)S(1)} %get-tuple-element.243, s32[]{:T(128)} %get-tuple-element.240, f32[128,8,1152]{2,0,1:T(8,128)} %fusion.173, bf16[4,128,8,128]{1,3,2,0:T(8,128)(2,1)} %get-tuple-element.258, f32[128,8,1152]{2,0,1:T(8,128)} %get-tuple-element.226, ...), kind=kOutput, calls=%fused_computation.17.clone.1 | convolution fusion | flops 310249600 | bytes 19735552 | tf_op jit(solution)/shard_map/while/body/eval_jaxpr/rhk,rhd->kd/dot_general | solution.py:53
  494.1 12.6 %fusion.174 = bf16[4,128,8,128]{3,1,2,0:T(8,128)(2,1)} fusion(bf16[4,128,8,128]{3,1,2,0:T(8,128)(2,1)} %get-tuple-element.242, s32[]{:T(128)} %get-tuple-element.240, f32[128,8,1152]{2,0,1:T(8,128)} %fusion.173, bf16[4,1152,128]{2,1,0:T(8,128)(2,1)} %get-tuple-element.259, f32[128,8,1152]{2,0,1:T(8,128)} %get-tuple-element.226, ...), kind=kOutput, calls=%fused_computation.28.clone.1 | convolution fusion | flops 310380672 | bytes 19440640 | tf_op jit(solution)/shard_map/while/body/eval_jaxpr/rhk,kd->rhd/dot_general | solution.py:50
  506.7 4.8 fusion.176
  511.5 5.1 fusion.172
  517.6 5.7 exponential_reduce_fusion.2
  523.3 3.9 fusion.173
  527.3 12.1 %fusion.175 = f32[4,1152,128]{1,2,0:T(8,128)S(1)} fusion(f32[4,1152,128]{1,2,0:T(8,128)S(1)} %get-tuple-element.243, s32[]{:T(128)} %get-tuple-element.240, f32[128,8,1152]{2,0,1:T(8,128)} %fusion.173, bf16[4,128,8,128]{1,3,2,0:T(8,128)(2,1)} %get-tuple-element.258, f32[128,8,1152]{2,0,1:T(8,128)} %get-tuple-element.226, ...), kind=kOutput, calls=%fused_computation.17.clone.1 | convolution fusion | flops 310249600 | bytes 19735552 | tf_op jit(solution)/shard_map/while/body/eval_jaxpr/rhk,rhd->kd/dot_general | solution.py:53
  539.4 12.6 %fusion.174 = bf16[4,128,8,128]{3,1,2,0:T(8,128)(2,1)} fusion(bf16[4,128,8,128]{3,1,2,0:T(8,128)(2,1)} %get-tuple-element.242, s32[]{:T(128)} %get-tuple-element.240, f32[128,8,1152]{2,0,1:T(8,128)} %fusion.173, bf16[4,1152,128]{2,1,0:T(8,128)(2,1)} %get-tuple-element.259, f32[128,8,1152]{2,0,1:T(8,128)} %get-tuple-element.226, ...), kind=kOutput, calls=%fused_computation.28.clone.1 | convolution fusion | flops 310380672 | bytes 19440640 | tf_op jit(solution)/shard_map/while/body/eval_jaxpr/rhk,kd->rhd/dot_general | solution.py:50
  552.0 4.8 fusion.176
  556.8 5.1 fusion.172
  561.9 2.0 fusion.108
  563.9 1.9 collective-permute-start.10
  565.8 4.3 collective-permute-start.11
  570.1 6.0 collective-permute-start.12
  576.1 2.0 collective-permute-start.13
  578.1 1.9 collective-permute-start.14
  580.1 1.9 collective-permute-done.10
  582.0 17.8 %collective-permute-start.15 = (f32[128,1024]{0,1:T(8,128)S(1)}, f32[128,1024]{0,1:T(8,128)S(1)}, u32[]{:S(2)}, u32[]{:S(2)}) collective-permute-start(f32[128,1024]{0,1:T(8,128)S(1)} %get-tuple-element.144), channel_id=1, source_target_pairs={{8,0},{9,1},{10,2},{11,3},{12,4},{13,5},{14,6},{15,7},{16,8},{17,9... | collective-permute-start | bytes 1572872 | tf_op jit(solution)/shard_map/ppermute | solution.py:26
  599.8 16.0 %collective-permute-done.11 = f32[128,1024]{0,1:T(8,128)S(1)} collective-permute-done((f32[128,1024]{0,1:T(8,128)S(1)}, f32[128,1024]{0,1:T(8,128)S(1)}, u32[]{:S(2)}, u32[]{:S(2)}) %collective-permute-start.11) | collective-permute-done | bytes 524320 | tf_op jit(solution)/shard_map/ppermute | solution.py:26
  615.8 17.9 %collective-permute-start.8 = (f32[128,1024]{0,1:T(8,128)S(1)}, f32[128,1024]{0,1:T(8,128)S(1)}, u32[]{:S(2)}, u32[]{:S(2)}) collective-permute-start(f32[128,1024]{0,1:T(8,128)S(1)} %get-tuple-element.138), channel_id=1, source_target_pairs={{1,0},{2,1},{3,2},{4,3},{5,4},{6,5},{7,6},{8,7},{9,8},{10,9},{11,1... | collective-permute-start | bytes 1572872 | tf_op jit(solution)/shard_map/ppermute | solution.py:26
  633.7 13.1 %collective-permute-start.9 = (f32[128,1024]{0,1:T(8,128)S(1)}, f32[128,1024]{0,1:T(8,128)S(1)}, u32[]{:S(2)}, u32[]{:S(2)}) collective-permute-start(f32[128,1024]{0,1:T(8,128)S(1)} %get-tuple-element.139), channel_id=1, source_target_pairs={{2,0},{3,1},{4,2},{5,3},{6,4},{7,5},{8,6},{9,7},{10,8},{11,9},{12,... | collective-permute-start | bytes 1572872 | tf_op jit(solution)/shard_map/ppermute | solution.py:26
  646.8 32.7 %collective-permute-done.13 = f32[128,1024]{0,1:T(8,128)S(1)} collective-permute-done((f32[128,1024]{0,1:T(8,128)S(1)}, f32[128,1024]{0,1:T(8,128)S(1)}, u32[]{:S(2)}, u32[]{:S(2)}) %collective-permute-start.13) | collective-permute-done | bytes 524320 | tf_op jit(solution)/shard_map/ppermute | solution.py:26
  679.6 7.6 collective-permute-done.14
  691.9 162.5 %all_to_all.21 = bf16[16,128,1024]{1,2,0:T(8,128)(2,1)S(1)} all-to-all(bf16[16,128,1024]{1,2,0:T(8,128)(2,1)S(1)} %stack.2), channel_id=1, replica_groups=mesh['seq'=16,'fsdp_0'=8,'fsdp_1'=2] {'fsdp_0','fsdp_1'}, dimensions={0} | all-to-all | bytes 8388608 | tf_op jit(solution)/shard_map/all_to_all | solution.py:116
  854.5 5.2 fusion.102
  859.8 2.0 copy.25
  865.3 14.1 %convolution_convert_fusion.1 = bf16[128,8192]{1,0:T(8,128)(2,1)} fusion(bf16[8192,1024]{1,0:T(8,128)(2,1)} %all-gather.5.cloned.1.call-done, f32[128,1024]{0,1:T(8,128)} %copy-done.5, f32[128,1024]{0,1:T(8,128)} %copy-done.4, f32[128,1024]{0,1:T(8,128)} %copy-done.3, f32[128,1024]{0,1:T(8,128)} %copy-done.2, f32[128,1024]{0,1:T(8,128)S(1)} %collective-permute-done.11, ...), kind=kOutput, calls=%fused_computation.83 | convolution fusion | flops 2150891520 | bytes 27787272 | tf_op jit(solution)/shard_map/dot_general | solution.py:110
  879.3 124.5 %all-reduce.2.cloned.1.call-done = f32[512,1024]{0,1:T(8,128)} async-done(((f32[512,1024]{0,1:T(8,128)}), f32[512,1024]{0,1:T(8,128)}) %all-reduce.2.cloned.1.call-update) | async-done | bytes 2097168 | tf_op jit(solution)/shard_map/psum | solution.py:121
  1003.9 2.9 copy.30
  (64 shorter events, 19.6 us)
Async XLA Ops:
  7.2 1.2 copy-start.9
  7.2 45.2 %all-gather.3.cloned.1.call-start = ((), (), s32[]{:S(2)}) async-start(), calls=%async_computation.2 | async-start | bytes 3145728 | tf_op jit(solution)/shard_map/all_gather | solution.py:19
  10.0 42.5 %copy-start.1 = (bf16[128,8192]{1,0:T(8,128)(2,1)S(1)}, bf16[128,8192]{1,0:T(8,128)(2,1)}, u32[]{:S(2)}) copy-start(bf16[128,8192]{1,0:T(8,128)(2,1)} %param.7) | copy-start | bytes 6291460
  10.0 262.5 %all-gather.5.cloned.1.call-start = ((), (), s32[]{:S(2)}) async-start(), calls=%async_computation.3 | async-start | bytes 18874368 | tf_op jit(solution)/shard_map/all_gather | solution.py:19
  58.8 631.4 %all-to-all-start.1 = ((bf16[128,16,512]{2,0,1:T(8,128)(2,1)}), bf16[128,16,512]{2,0,1:T(8,128)(2,1)}, u32[]{:S(2)}, u32[]{:S(2)}) async-start(bf16[128,16,512]{2,0,1:T(8,128)(2,1)} %copy.29), calls=%async_computation.1 | async-start | bytes 4194304 | tf_op jit(solution)/shard_map/all_to_all | solution.py:84
  65.7 938.2 %all-reduce.2.cloned.1.call-start = ((), (), s32[]{:S(2)}) async-start(), calls=%async_computation.4 | async-start | bytes 4194304 | tf_op jit(solution)/shard_map/psum | solution.py:121
  280.6 26.5 %collective-permute-start = (bf16[128,1024]{1,0:T(8,128)(2,1)S(1)}, bf16[128,1024]{1,0:T(8,128)(2,1)}, u32[]{:S(2)}, u32[]{:S(2)}) collective-permute-start(bf16[128,1024]{1,0:T(8,128)(2,1)S(1)} %fusion.105), channel_id=1, source_target_pairs={{0,8},{1,9},{2,10},{3,11},{4,12},{5,13},{6,14},{7,15},{8,16},{9,17... | collective-permute-start | bytes 786440 | tf_op jit(solution)/shard_map/ppermute | solution.py:26
  285.5 28.2 %collective-permute-start.1 = (bf16[128,1024]{1,0:T(8,128)(2,1)S(1)}, bf16[128,1024]{1,0:T(8,128)(2,1)S(1)}, u32[]{:S(2)}, u32[]{:S(2)}) collective-permute-start(bf16[128,1024]{1,0:T(8,128)(2,1)S(1)} %fusion.105), channel_id=1, source_target_pairs={{0,7},{1,8},{2,9},{3,10},{4,11},{5,12},{6,13},{7,14},{8,15},{9,16}... | collective-permute-start | bytes 786440 | tf_op jit(solution)/shard_map/ppermute | solution.py:26
  289.5 45.6 %collective-permute-start.2 = (bf16[128,1024]{1,0:T(8,128)(2,1)S(1)}, bf16[128,1024]{1,0:T(8,128)(2,1)S(1)}, u32[]{:S(2)}, u32[]{:S(2)}) collective-permute-start(bf16[128,1024]{1,0:T(8,128)(2,1)S(1)} %fusion.105), channel_id=1, source_target_pairs={{0,6},{1,7},{2,8},{3,9},{4,10},{5,11},{6,12},{7,13},{8,14},{9,15},... | collective-permute-start | bytes 786440 | tf_op jit(solution)/shard_map/ppermute | solution.py:26
  300.2 52.2 %collective-permute-start.3 = (bf16[128,1024]{1,0:T(8,128)(2,1)S(1)}, bf16[128,1024]{1,0:T(8,128)(2,1)S(1)}, u32[]{:S(2)}, u32[]{:S(2)}) collective-permute-start(bf16[128,1024]{1,0:T(8,128)(2,1)S(1)} %fusion.105), channel_id=1, source_target_pairs={{0,5},{1,6},{2,7},{3,8},{4,9},{5,10},{6,11},{7,12},{8,13},{9,14},{... | collective-permute-start | bytes 786440 | tf_op jit(solution)/shard_map/ppermute | solution.py:26
  304.8 47.6 %collective-permute-start.4 = (bf16[128,1024]{1,0:T(8,128)(2,1)S(1)}, bf16[128,1024]{1,0:T(8,128)(2,1)S(1)}, u32[]{:S(2)}, u32[]{:S(2)}) collective-permute-start(bf16[128,1024]{1,0:T(8,128)(2,1)S(1)} %fusion.105), channel_id=1, source_target_pairs={{0,4},{1,5},{2,6},{3,7},{4,8},{5,9},{6,10},{7,11},{8,12},{9,13},{1... | collective-permute-start | bytes 786440 | tf_op jit(solution)/shard_map/ppermute | solution.py:26
  307.0 51.3 %collective-permute-start.5 = (bf16[128,1024]{1,0:T(8,128)(2,1)S(1)}, bf16[128,1024]{1,0:T(8,128)(2,1)S(1)}, u32[]{:S(2)}, u32[]{:S(2)}) collective-permute-start(bf16[128,1024]{1,0:T(8,128)(2,1)S(1)} %fusion.105), channel_id=1, source_target_pairs={{0,3},{1,4},{2,5},{3,6},{4,7},{5,8},{6,9},{7,10},{8,11},{9,12},{10... | collective-permute-start | bytes 786440 | tf_op jit(solution)/shard_map/ppermute | solution.py:26
  313.7 52.9 %collective-permute-start.6 = (bf16[128,1024]{1,0:T(8,128)(2,1)S(1)}, bf16[128,1024]{1,0:T(8,128)(2,1)S(1)}, u32[]{:S(2)}, u32[]{:S(2)}) collective-permute-start(bf16[128,1024]{1,0:T(8,128)(2,1)S(1)} %fusion.105), channel_id=1, source_target_pairs={{0,2},{1,3},{2,4},{3,5},{4,6},{5,7},{6,8},{7,9},{8,10},{9,11},{10,... | collective-permute-start | bytes 786440 | tf_op jit(solution)/shard_map/ppermute | solution.py:26
  335.1 43.8 %collective-permute-start.7 = (bf16[128,1024]{1,0:T(8,128)(2,1)S(1)}, bf16[128,1024]{1,0:T(8,128)(2,1)S(1)}, u32[]{:S(2)}, u32[]{:S(2)}) collective-permute-start(bf16[128,1024]{1,0:T(8,128)(2,1)S(1)} %fusion.105), channel_id=1, source_target_pairs={{0,1},{1,2},{2,3},{3,4},{4,5},{5,6},{6,7},{7,8},{8,9},{9,10},{10,1... | collective-permute-start | bytes 786440 | tf_op jit(solution)/shard_map/ppermute | solution.py:26
  561.9 127.1 %copy-start = (f32[4,1152,128]{1,2,0:T(8,128)S(1)}, f32[4,1152,128]{1,2,0:T(8,128)}, u32[]{:S(2)}) copy-start(f32[4,1152,128]{1,2,0:T(8,128)} %get-tuple-element.62) | copy-start | bytes 7077892
  563.9 18.1 %collective-permute-start.10 = (f32[128,1024]{0,1:T(8,128)S(1)}, f32[128,1024]{0,1:T(8,128)S(1)}, u32[]{:S(2)}, u32[]{:S(2)}) collective-permute-start(f32[128,1024]{0,1:T(8,128)S(1)} %get-tuple-element.140), channel_id=1, source_target_pairs={{3,0},{4,1},{5,2},{6,3},{7,4},{8,5},{9,6},{10,7},{11,8},{12,9},{13... | collective-permute-start | bytes 1572872 | tf_op jit(solution)/shard_map/ppermute | solution.py:26
  565.8 50.0 %collective-permute-start.11 = (f32[128,1024]{0,1:T(8,128)S(1)}, f32[128,1024]{0,1:T(8,128)S(1)}, u32[]{:S(2)}, u32[]{:S(2)}) collective-permute-start(f32[128,1024]{0,1:T(8,128)S(1)} %get-tuple-element.141), channel_id=1, source_target_pairs={{4,0},{5,1},{6,2},{7,3},{8,4},{9,5},{10,6},{11,7},{12,8},{13,9},{1... | collective-permute-start | bytes 1572872 | tf_op jit(solution)/shard_map/ppermute | solution.py:26
  570.1 63.6 %collective-permute-start.12 = (f32[128,1024]{0,1:T(8,128)S(1)}, f32[128,1024]{0,1:T(8,128)S(1)}, u32[]{:S(2)}, u32[]{:S(2)}) collective-permute-start(f32[128,1024]{0,1:T(8,128)S(1)} %get-tuple-element.142), channel_id=1, source_target_pairs={{5,0},{6,1},{7,2},{8,3},{9,4},{10,5},{11,6},{12,7},{13,8},{14,9},{... | collective-permute-start | bytes 1572872 | tf_op jit(solution)/shard_map/ppermute | solution.py:26
  576.1 103.4 %collective-permute-start.13 = (f32[128,1024]{0,1:T(8,128)S(1)}, f32[128,1024]{0,1:T(8,128)S(1)}, u32[]{:S(2)}, u32[]{:S(2)}) collective-permute-start(f32[128,1024]{0,1:T(8,128)S(1)} %get-tuple-element.143), channel_id=1, source_target_pairs={{6,0},{7,1},{8,2},{9,3},{10,4},{11,5},{12,6},{13,7},{14,8},{15,9},... | collective-permute-start | bytes 1572872 | tf_op jit(solution)/shard_map/ppermute | solution.py:26
  578.1 109.0 %collective-permute-start.14 = (f32[128,1024]{0,1:T(8,128)S(1)}, f32[128,1024]{0,1:T(8,128)S(1)}, u32[]{:S(2)}, u32[]{:S(2)}) collective-permute-start(f32[128,1024]{0,1:T(8,128)S(1)} %get-tuple-element.145), channel_id=1, source_target_pairs={{7,0},{8,1},{9,2},{10,3},{11,4},{12,5},{13,6},{14,7},{15,8},{16,9}... | collective-permute-start | bytes 1572872 | tf_op jit(solution)/shard_map/ppermute | solution.py:26
  582.0 105.2 %collective-permute-start.15 = (f32[128,1024]{0,1:T(8,128)S(1)}, f32[128,1024]{0,1:T(8,128)S(1)}, u32[]{:S(2)}, u32[]{:S(2)}) collective-permute-start(f32[128,1024]{0,1:T(8,128)S(1)} %get-tuple-element.144), channel_id=1, source_target_pairs={{8,0},{9,1},{10,2},{11,3},{12,4},{13,5},{14,6},{15,7},{16,8},{17,9... | collective-permute-start | bytes 1572872 | tf_op jit(solution)/shard_map/ppermute | solution.py:26
  615.8 71.4 %collective-permute-start.8 = (f32[128,1024]{0,1:T(8,128)S(1)}, f32[128,1024]{0,1:T(8,128)S(1)}, u32[]{:S(2)}, u32[]{:S(2)}) collective-permute-start(f32[128,1024]{0,1:T(8,128)S(1)} %get-tuple-element.138), channel_id=1, source_target_pairs={{1,0},{2,1},{3,2},{4,3},{5,4},{6,5},{7,6},{8,7},{9,8},{10,9},{11,1... | collective-permute-start | bytes 1572872 | tf_op jit(solution)/shard_map/ppermute | solution.py:26
  633.7 53.5 %copy-start.2 = (f32[128,1024]{0,1:T(8,128)}, f32[128,1024]{0,1:T(8,128)S(1)}, u32[]{:S(2)}) copy-start(f32[128,1024]{0,1:T(8,128)S(1)} %collective-permute-done.12) | copy-start | bytes 1572868
  633.7 53.5 %collective-permute-start.9 = (f32[128,1024]{0,1:T(8,128)S(1)}, f32[128,1024]{0,1:T(8,128)S(1)}, u32[]{:S(2)}, u32[]{:S(2)}) collective-permute-start(f32[128,1024]{0,1:T(8,128)S(1)} %get-tuple-element.139), channel_id=1, source_target_pairs={{2,0},{3,1},{4,2},{5,3},{6,4},{7,5},{8,6},{9,7},{10,8},{11,9},{12,... | collective-permute-start | bytes 1572872 | tf_op jit(solution)/shard_map/ppermute | solution.py:26
  679.6 7.6 copy-start.3
  687.2 0.8 copy-start.4
  687.2 1.0 copy-start.5
  687.2 1.1 copy-start.6
  688.3 0.8 copy-start.7
  859.7 3.4 copy-start.8
Sparse Core Ops, SparseCore 0:
  10.4 41.9 all-gather.2
  54.2 218.1 all-gather.4
  859.8 143.9 all-reduce.1
